TPU v7x, 512 devices: a whole 4x4x16 slice. The times are simulated.
512 devices in a mesh: dp: 8 (over x, z_hi), expert: 64 (over y, z_lo, core).
Axes of the slice: x: 4, y: 4, z: 16 (z_hi: 2, z_lo: 8; z = z_hi * 8 + z_lo), core: 2. Of those that a mesh axis runs over, the one named last changes fastest.
Arguments:
- tokens: bfloat16 [2, 4096, 2048], P(None, 'expert', 'dp'), may hold values from -6 to 6
- cotangent: bfloat16 [2, 4096, 2048], P(None, 'expert', 'dp'), may hold values from -6 to 6
- routes: int32 [2, 4096, 2], P(None, 'expert'), may hold values from 0 to 63, all different within a row; in each aligned block of 64 rows (0 to 63, 64 to 127, ..., all dimensions but the last counted through in order) at most 3 rows name the same one
- gates: float32 [2, 4096, 2], P(None, 'expert'), may hold values from 0.25 to 1
- source: int32 [64], replicated, may hold values from 0 to 63, as said below
- w_gate_up: bfloat16 [64, 2048, 2, 1024], P('expert', None, None, 'dp'), may hold values from -0.125 to 0.125
- w_down: bfloat16 [64, 1024, 2048], P('expert', 'dp'), may hold values from -0.1875 to 0.1875
- moment_first: bfloat16 [64, 1024, 2048], P('expert', 'dp'), may hold values from -6 to 6
- moment_second: bfloat16 [64, 1024, 2048], P('expert', 'dp'), may hold values from 0.25 to 4
Outputs:
- layer_out: bfloat16 [2, 4096, 2048], P(None, 'expert', 'dp')
- token_grad: bfloat16 [2, 4096, 2048], P(None, 'expert', 'dp')
- update_dir: bfloat16 [64, 1024, 2048], P('expert', 'dp')
- new_first: bfloat16 [64, 1024, 2048], P('expert', 'dp')
- new_second: bfloat16 [64, 1024, 2048], P('expert', 'dp')
Inputs may be any that keep to these rules, and one draw needn't show every extreme that they name: `routes`: in each micro-batch, the 64 tokens of one index of expert name no expert more than 3 times, a bound that some block reaches. source[source[s]] = s for every slot; 32 slots take another slot's expert.
All inputs are finite; a program needn't handle non-finite values.
Results may differ from a plain program's by a relative error of at most 0.018.
Values may be sent and summed in bfloat16 or wider, within the bound.
A program may use at most 64 MiB of HBM per device.

v0:
```python
import jax
import jax.numpy as jnp
from jax import lax
from jax.sharding import PartitionSpec as P

contract_first = (((0,), (0,)), ((), ()))
contract_second = (((1,), (1,)), ((), ()))


def split_back(flattened, templates):
    outputs = []
    offset = 0
    for template in templates:
        element_count = template.size
        outputs.append(flattened[offset : offset + element_count].reshape(template.shape))
        offset = offset + element_count
    return outputs


def relocate_state(arrays, source, experts):
    flattened = jnp.concatenate([member.reshape(-1) for member in arrays]).reshape(experts, -1)
    spread = lax.all_to_all(flattened, "expert", split_axis=0, concat_axis=0, tiled=True)
    picked = jnp.take(spread, source, axis=0)
    final = lax.all_to_all(picked, "expert", split_axis=0, concat_axis=0, tiled=True)
    return split_back(final.reshape(-1), arrays)


def per_device(
    tokens, cotangent, routes, gates, source, w_gate_up, w_down, moment_first, moment_second
):
    experts = lax.axis_size("expert")
    micro_count, token_count, part_width = tokens.shape
    model_width = w_gate_up.shape[1]
    hidden_part = w_gate_up.shape[3]
    top_count = routes.shape[2]
    capacity = max(2, 3 * token_count * top_count // (2 * experts))
    slots = experts * capacity
    column_ids = jnp.arange(experts, dtype=jnp.int32)
    w_gate_up, w_down, moment_first, moment_second = relocate_state(
        (w_gate_up, w_down, moment_first, moment_second), source, experts
    )
    target = jnp.sum(jnp.where(routes[..., None] == column_ids, source, 0), axis=-1)
    slot_ids = jnp.arange(slots, dtype=jnp.int32)
    picks_list = []
    plain_list = []
    slot_gate_list = []
    for micro in range(micro_count):
        chosen = target[micro].reshape(-1)
        onehot = (chosen[:, None] == column_ids).astype(jnp.int32)
        position = jnp.sum((jnp.cumsum(onehot, axis=0) - onehot) * onehot, axis=1)
        slot_of = (chosen * capacity + position).reshape(token_count, top_count)
        picks = []
        slot_gate = jnp.zeros((slots,), jnp.float32)
        for choice_k in range(top_count):
            match = slot_of[:, choice_k][:, None] == slot_ids
            picks.append(match.astype(jnp.bfloat16))
            slot_gate = slot_gate + jnp.sum(
                jnp.where(match, gates[micro][:, choice_k : choice_k + 1], 0.0), axis=0
            )
        plain = picks[0]
        choice_k = 1
        plain = plain + picks[choice_k]
        picks_list.append(picks)
        plain_list.append(plain)
        slot_gate_list.append(slot_gate)
    gate_up_flat = w_gate_up.reshape(model_width, 2 * hidden_part)
    down_local = w_down.reshape(hidden_part, model_width)
    source_tokens, source_grads = (
        lax.all_gather(tokens, "dp", axis=2, tiled=True),
        lax.all_gather(cotangent, "dp", axis=2, tiled=True),
    )
    down_grad = jnp.zeros((hidden_part, model_width), jnp.float32)
    layer_parts = []
    grad_parts = []
    for micro in range(micro_count):
        plain = plain_list[micro]
        picks = picks_list[micro]
        slot_gate = slot_gate_list[micro]
        row_tokens = lax.dot_general(
            plain, source_tokens[micro], contract_first, preferred_element_type=jnp.float32
        ).astype(jnp.bfloat16)
        row_grads = (
            lax.dot_general(
                plain, source_grads[micro], contract_first, preferred_element_type=jnp.float32
            )
            * slot_gate[:, None]
        ).astype(jnp.bfloat16)
        send_width = row_tokens.shape[1]
        arrived_tokens, arrived_grads = (
            lax.all_to_all(
                row_tokens.reshape(experts, capacity, send_width),
                "expert",
                split_axis=0,
                concat_axis=0,
                tiled=True,
            ),
            lax.all_to_all(
                row_grads.reshape(experts, capacity, send_width),
                "expert",
                split_axis=0,
                concat_axis=0,
                tiled=True,
            ),
        )
        expert_in = arrived_tokens.reshape(slots, model_width)
        grad_in = arrived_grads.reshape(slots, model_width)
        both = jnp.dot(expert_in, gate_up_flat, preferred_element_type=jnp.float32).reshape(
            slots, 2, hidden_part
        )
        gate_pre = both[:, 0]
        up_pre = both[:, 1]
        gate_sig = jax.nn.sigmoid(gate_pre)
        hidden = (gate_pre * gate_sig * up_pre).astype(jnp.bfloat16)
        partial_out = jnp.dot(hidden, down_local, preferred_element_type=jnp.float32)
        summed_out = lax.psum_scatter(
            partial_out.reshape(experts, capacity, model_width).astype(jnp.bfloat16),
            "dp",
            scatter_dimension=2,
            tiled=True,
        )
        returned_out = lax.all_to_all(summed_out, "expert", split_axis=0, concat_axis=0, tiled=True)
        returned_out = returned_out.reshape(slots, -1)
        combined = jnp.zeros((token_count, returned_out.shape[1]), jnp.float32)
        for choice_k in range(top_count):
            combined = combined + gates[micro][:, choice_k : choice_k + 1] * jnp.dot(
                picks[choice_k], returned_out, preferred_element_type=jnp.float32
            )
        layer_parts.append(combined.astype(jnp.bfloat16))
        hidden_grad = lax.dot_general(
            grad_in, down_local, contract_second, preferred_element_type=jnp.float32
        )
        down_grad = down_grad + lax.dot_general(
            hidden, grad_in, contract_first, preferred_element_type=jnp.float32
        )
        gate_grad = hidden_grad * up_pre * gate_sig * (1.0 + gate_pre * (1.0 - gate_sig))
        up_grad = hidden_grad * gate_pre * gate_sig
        both_grad = (
            jnp.stack([gate_grad, up_grad], axis=1)
            .astype(jnp.bfloat16)
            .reshape(slots, 2 * hidden_part)
        )
        partial_in = lax.dot_general(
            both_grad, gate_up_flat, contract_second, preferred_element_type=jnp.float32
        )
        summed_in = lax.psum_scatter(
            partial_in.reshape(experts, capacity, model_width).astype(jnp.bfloat16),
            "dp",
            scatter_dimension=2,
            tiled=True,
        )
        returned_in = lax.all_to_all(summed_in, "expert", split_axis=0, concat_axis=0, tiled=True)
        returned_in = returned_in.reshape(slots, -1)
        gathered = jnp.zeros((token_count, returned_in.shape[1]), jnp.float32)
        for choice_k in range(top_count):
            gathered = gathered + jnp.dot(
                picks[choice_k], returned_in, preferred_element_type=jnp.float32
            )
        grad_parts.append(gathered.astype(jnp.bfloat16))
    first = (
        0.9 * moment_first.reshape(hidden_part, model_width).astype(jnp.float32) + 0.1 * down_grad
    )
    second = (
        0.999 * moment_second.reshape(hidden_part, model_width).astype(jnp.float32)
        + 0.001 * down_grad * down_grad
    )
    update = first / (jnp.sqrt(second) + 1e-08)
    results = (
        update.astype(jnp.bfloat16).reshape(moment_first.shape),
        first.astype(jnp.bfloat16).reshape(moment_first.shape),
        second.astype(jnp.bfloat16).reshape(moment_first.shape),
    )
    return (jnp.stack(layer_parts), jnp.stack(grad_parts), results[0], results[1], results[2])


def solution(mesh):
    placed = (
        P(None, "expert", "dp"),
        P(None, "expert", "dp"),
        P(None, "expert", None),
        P(None, "expert", None),
        P(),
        P("expert", None, None, "dp"),
        P("expert", "dp", None),
        P("expert", "dp", None),
        P("expert", "dp", None),
    )
    return jax.shard_map(
        per_device,
        mesh=mesh,
        in_specs=placed,
        out_specs=(
            P(None, "expert", "dp"),
            P(None, "expert", "dp"),
            P("expert", "dp", None),
            P("expert", "dp", None),
            P("expert", "dp", None),
        ),
        check_vma=False,
    )
```

profile of v0, /device:TPU:1, one launch (start us, length us, event | category | flops | bytes accessed | tf_op | source)
XLA Modules:
  0.0 1163.6 jit_solution(4076985666100060504)
XLA Ops:
  10.7 16.8 %pad_maximum_fusion = bf16[1310720]{0:T(1024)(128)(2,1)S(1)} fusion(bf16[262144]{0:T(1024)(128)(2,1)S(1)} %bitcast.190, bf16[262144]{0:T(1024)(128)(2,1)S(1)} %bitcast.191, bf16[262144]{0:T(1024)(128)(2,1)S(1)} %bitcast.192, bf16[524288]{0:T(1024)(128)(2,1)S(1)} %bitcast.193), kind=kLoop, calls=%fused_computation.1 | loop fusion | flops 10485760 | bytes 5242880 | tf_op jit(solution)/shard_map/concatenate | solution.py:21
  34.6 16.1 %reduce.2 = bf16[64,20480]{1,0:T(8,128)(2,1)S(1)} reduce(bf16[64,1,20480]{2,1,0:T(2,128)(2,1)} %all_to_all.48, bf16[]{:T(256)} %broadcast.97), dimensions={1}, to_apply=%all_to_all.48.reduce_sub_computation | reduce | bytes 5242882 | tf_op jit(solution)/shard_map/all_to_all | solution.py:22
  53.8 17.5 %all-to-all-start.1 = ((bf16[64,2,10240]{2,1,0:T(2,128)(2,1)}), bf16[64,2,10240]{2,1,0:T(2,128)(2,1)S(1)}, u32[]{:S(2)}, u32[]{:S(2)}) async-start(bf16[64,2,10240]{2,1,0:T(2,128)(2,1)} %reshape.197), calls=%async_computation.1 | async-start | bytes 5242880 | tf_op jit(solution)/shard_map/all_to_all | solution.py:22
  73.5 107.9 %all_gather.6 = bf16[2,64,2048]{2,1,0:T(8,128)(2,1)S(1)} all-gather(bf16[2,64,256]{2,1,0:T(8,128)(2,1)S(1)} %copy-done.11), channel_id=1, replica_groups=mesh['dp'=8,'expert'=64] {'dp'}, dimensions={2}, use_global_device_ids=true | all-gather | bytes 589824 | tf_op jit(solution)/shard_map/all_gather | solution.py:69
  184.0 34.8 %all-to-all-done.1 = bf16[64,2,10240]{2,1,0:T(2,128)(2,1)S(1)} async-done(((bf16[64,2,10240]{2,1,0:T(2,128)(2,1)}), bf16[64,2,10240]{2,1,0:T(2,128)(2,1)S(1)}, u32[]{:S(2)}, u32[]{:S(2)}) %all-to-all-start.1) | async-done | bytes 2621472 | tf_op jit(solution)/shard_map/all_to_all | solution.py:22
  218.8 58.5 %all-to-all-start.4 = ((bf16[64,3,2048]{2,1,0:T(4,128)(2,1)}), bf16[64,3,2048]{2,1,0:T(4,128)(2,1)}, u32[]{:S(2)}, u32[]{:S(2)}) async-start(bf16[64,3,2048]{2,1,0:T(4,128)(2,1)} %reshape.168), calls=%async_computation.5 | async-start | bytes 2097152 | tf_op jit(solution)/shard_map/all_to_all | solution.py:90
  277.6 69.5 %all_gather.7 = bf16[2,64,2048]{2,1,0:T(8,128)(2,1)S(1)} all-gather(bf16[2,64,256]{2,1,0:T(8,128)(2,1)S(1)} %copy-done.12), channel_id=1, replica_groups=mesh['dp'=8,'expert'=64] {'dp'}, dimensions={2}, use_global_device_ids=true | all-gather | bytes 589824 | tf_op jit(solution)/shard_map/all_gather | solution.py:70
  365.9 61.2 %all-to-all-start.8 = ((bf16[64,3,2048]{2,1,0:T(4,128)(2,1)}), bf16[64,3,2048]{2,1,0:T(4,128)(2,1)}, u32[]{:S(2)}, u32[]{:S(2)}) async-start(bf16[64,3,2048]{2,1,0:T(4,128)(2,1)} %reshape.174), calls=%async_computation.11 | async-start | bytes 2097152 | tf_op jit(solution)/shard_map/all_to_all | solution.py:97
  438.3 39.9 %all-to-all-done.8 = bf16[64,3,2048]{2,1,0:T(4,128)(2,1)} async-done(((bf16[64,3,2048]{2,1,0:T(4,128)(2,1)}), bf16[64,3,2048]{2,1,0:T(4,128)(2,1)}, u32[]{:S(2)}, u32[]{:S(2)}) %all-to-all-start.8) | async-done | bytes 786464 | tf_op jit(solution)/shard_map/all_to_all | solution.py:97
  478.2 8.1 all-to-all-start.2
  489.0 115.7 %all-to-all-done.2 = bf16[64,2,10240]{2,1,0:T(2,128)(2,1)S(1)} async-done(((bf16[64,2,10240]{2,1,0:T(2,128)(2,1)}), bf16[64,2,10240]{2,1,0:T(2,128)(2,1)S(1)}, u32[]{:S(2)}, u32[]{:S(2)}) %all-to-all-start.2) | async-done | bytes 2621472 | tf_op jit(solution)/shard_map/all_to_all | solution.py:24
  604.8 8.6 all-to-all-start
  623.1 15.5 %reduce = bf16[64,20480]{1,0:T(8,128)(2,1)S(1)} reduce(bf16[64,1,20480]{2,1,0:T(2,128)(2,1)} %reshape.200, bf16[]{:T(256)} %constant.43), dimensions={1}, to_apply=%all_to_all.40.reduce_sub_computation | reduce | bytes 5242882 | tf_op jit(solution)/shard_map/all_to_all | solution.py:24
  655.8 8.9 all-to-all-done
  664.6 8.3 all-to-all-start.6
  685.1 52.7 %all-to-all-done.6 = bf16[64,3,2048]{2,1,0:T(4,128)(2,1)} async-done(((bf16[64,3,2048]{2,1,0:T(4,128)(2,1)}), bf16[64,3,2048]{2,1,0:T(4,128)(2,1)}, u32[]{:S(2)}, u32[]{:S(2)}) %all-to-all-start.6) | async-done | bytes 786464 | tf_op jit(solution)/shard_map/all_to_all | solution.py:97
  744.8 33.3 %reduce-scatter.7.cloned.1.call-done = bf16[64,3,256]{2,0,1:T(8,128)(2,1)} async-done(((bf16[64,3,2048]{2,0,1:T(8,128)(2,1)}), bf16[64,3,256]{2,0,1:T(8,128)(2,1)}) %reduce-scatter.7.cloned.1.call-update) | async-done | bytes 98320 | tf_op jit(solution)/shard_map/reduce_scatter | solution.py:115
  787.3 101.6 %reduce-scatter.11.cloned.1.call-done = bf16[64,3,256]{2,0,1:T(8,128)(2,1)} async-done(((bf16[64,3,2048]{2,0,1:T(8,128)(2,1)}), bf16[64,3,256]{2,0,1:T(8,128)(2,1)}) %reduce-scatter.11.cloned.1.call-update) | async-done | bytes 98320 | tf_op jit(solution)/shard_map/reduce_scatter | solution.py:145
  890.5 7.5 all-to-all-start.9
  902.7 97.1 %reduce-scatter.5.cloned.1.call-done = bf16[64,3,256]{2,0,1:T(8,128)(2,1)} async-done(((bf16[64,3,2048]{2,0,1:T(8,128)(2,1)}), bf16[64,3,256]{2,0,1:T(8,128)(2,1)}) %reduce-scatter.5.cloned.1.call-update) | async-done | bytes 98320 | tf_op jit(solution)/shard_map/reduce_scatter | solution.py:115
  1001.5 108.9 %reduce-scatter.9.cloned.1.call-done = bf16[64,3,256]{2,0,1:T(8,128)(2,1)} async-done(((bf16[64,3,2048]{2,0,1:T(8,128)(2,1)}), bf16[64,3,256]{2,0,1:T(8,128)(2,1)}) %reduce-scatter.9.cloned.1.call-update) | async-done | bytes 98320 | tf_op jit(solution)/shard_map/reduce_scatter | solution.py:145
  1112.1 7.5 all-to-all-start.3
  1120.4 13.9 %all-to-all-done.3 = bf16[64,3,256]{2,1,0:T(4,128)(2,1)S(1)} async-done(((bf16[64,3,256]{2,1,0:T(4,128)(2,1)}), bf16[64,3,256]{2,1,0:T(4,128)(2,1)S(1)}, u32[]{:S(2)}, u32[]{:S(2)}) %all-to-all-start.3) | async-done | bytes 98336 | tf_op jit(solution)/shard_map/all_to_all | solution.py:121
  1141.1 13.9 %all-to-all-done.7 = bf16[64,3,256]{2,1,0:T(4,128)(2,1)S(1)} async-done(((bf16[64,3,256]{2,1,0:T(4,128)(2,1)}), bf16[64,3,256]{2,1,0:T(4,128)(2,1)S(1)}, u32[]{:S(2)}, u32[]{:S(2)}) %all-to-all-start.7) | async-done | bytes 98336 | tf_op jit(solution)/shard_map/all_to_all | solution.py:151
  (160 shorter events, 124.9 us)
Async XLA Ops:
  53.8 164.9 %all-to-all-start.1 = ((bf16[64,2,10240]{2,1,0:T(2,128)(2,1)}), bf16[64,2,10240]{2,1,0:T(2,128)(2,1)S(1)}, u32[]{:S(2)}, u32[]{:S(2)}) async-start(bf16[64,2,10240]{2,1,0:T(2,128)(2,1)} %reshape.197), calls=%async_computation.1 | async-start | bytes 5242880 | tf_op jit(solution)/shard_map/all_to_all | solution.py:22
  181.4 95.9 %copy-start.22 = (f32[2,64,2]{1,2,0:T(2,128)S(1)}, f32[2,64,2]{1,2,0:T(2,128)}, u32[]{:S(2)}) copy-start(f32[2,64,2]{1,2,0:T(2,128)} %param.12) | copy-start | bytes 3076
  181.4 96.2 %copy-start.12 = (bf16[2,64,256]{2,1,0:T(8,128)(2,1)S(1)}, bf16[2,64,256]{2,1,0:T(8,128)(2,1)}, u32[]{:S(2)}) copy-start(bf16[2,64,256]{2,1,0:T(8,128)(2,1)} %param.10) | copy-start | bytes 196612
  218.8 147.1 %all-to-all-start.4 = ((bf16[64,3,2048]{2,1,0:T(4,128)(2,1)}), bf16[64,3,2048]{2,1,0:T(4,128)(2,1)}, u32[]{:S(2)}, u32[]{:S(2)}) async-start(bf16[64,3,2048]{2,1,0:T(4,128)(2,1)} %reshape.168), calls=%async_computation.5 | async-start | bytes 2097152 | tf_op jit(solution)/shard_map/all_to_all | solution.py:90
  277.4 79.5 %copy-start.13 = (f32[64]{0:T(128)}, f32[64]{0:T(128)S(1)}, u32[]{:S(2)}) copy-start(f32[64]{0:T(128)S(1)} %get-tuple-element.26) | copy-start | bytes 772
  277.4 79.5 %copy-start.15 = (f32[64]{0:T(128)}, f32[64]{0:T(128)S(1)}, u32[]{:S(2)}) copy-start(f32[64]{0:T(128)S(1)} %get-tuple-element.27) | copy-start | bytes 772
  365.9 112.3 %all-to-all-start.8 = ((bf16[64,3,2048]{2,1,0:T(4,128)(2,1)}), bf16[64,3,2048]{2,1,0:T(4,128)(2,1)}, u32[]{:S(2)}, u32[]{:S(2)}) async-start(bf16[64,3,2048]{2,1,0:T(4,128)(2,1)} %reshape.174), calls=%async_computation.11 | async-start | bytes 2097152 | tf_op jit(solution)/shard_map/all_to_all | solution.py:97
  478.2 126.6 %all-to-all-start.2 = ((bf16[64,2,10240]{2,1,0:T(2,128)(2,1)}), bf16[64,2,10240]{2,1,0:T(2,128)(2,1)S(1)}, u32[]{:S(2)}, u32[]{:S(2)}) async-start(bf16[64,2,10240]{2,1,0:T(2,128)(2,1)} %reshape.199), calls=%async_computation.2 | async-start | bytes 5242880 | tf_op jit(solution)/shard_map/all_to_all | solution.py:24
  604.8 59.9 %all-to-all-start = ((bf16[64,3,2048]{2,1,0:T(4,128)(2,1)}), bf16[64,3,2048]{2,1,0:T(4,128)(2,1)}, u32[]{:S(2)}, u32[]{:S(2)}) async-start(bf16[64,3,2048]{2,1,0:T(4,128)(2,1)} %reshape.161), calls=%async_computation | async-start | bytes 2097152 | tf_op jit(solution)/shard_map/all_to_all | solution.py:90
  613.4 164.7 %reduce-scatter.7.cloned.1.call-start = ((), (), s32[]{:S(2)}) async-start(), calls=%async_computation.15 | async-start | bytes 884736 | tf_op jit(solution)/shard_map/reduce_scatter | solution.py:115
  664.6 73.2 %all-to-all-start.6 = ((bf16[64,3,2048]{2,1,0:T(4,128)(2,1)}), bf16[64,3,2048]{2,1,0:T(4,128)(2,1)}, u32[]{:S(2)}, u32[]{:S(2)}) async-start(bf16[64,3,2048]{2,1,0:T(4,128)(2,1)} %reshape.171), calls=%async_computation.8 | async-start | bytes 2097152 | tf_op jit(solution)/shard_map/all_to_all | solution.py:97
  673.0 215.9 %reduce-scatter.11.cloned.1.call-start = ((), (), s32[]{:S(2)}) async-start(), calls=%async_computation.17 | async-start | bytes 884736 | tf_op jit(solution)/shard_map/reduce_scatter | solution.py:145
  677.7 322.1 %reduce-scatter.5.cloned.1.call-start = ((), (), s32[]{:S(2)}) async-start(), calls=%async_computation.14 | async-start | bytes 884736 | tf_op jit(solution)/shard_map/reduce_scatter | solution.py:115
  685.1 425.4 %reduce-scatter.9.cloned.1.call-start = ((), (), s32[]{:S(2)}) async-start(), calls=%async_computation.16 | async-start | bytes 884736 | tf_op jit(solution)/shard_map/reduce_scatter | solution.py:145
  744.8 154.6 %copy-start.8 = (bf16[192,2048]{1,0:T(8,128)(2,1)S(1)}, bf16[192,2048]{1,0:T(8,128)(2,1)}, u32[]{:S(2)}) copy-start(bf16[192,2048]{1,0:T(8,128)(2,1)} %copy-done.7) | copy-start | bytes 2359300
  744.8 154.6 %copy-start.10 = (f32[192,2,128]{2,0,1:T(8,128)S(1)}, f32[192,2,128]{2,0,1:T(8,128)}, u32[]{:S(2)}) copy-start(f32[192,2,128]{2,0,1:T(8,128)} %copy-done.9) | copy-start | bytes 589828
  779.7 110.8 %all-to-all-start.5 = ((bf16[64,3,256]{2,1,0:T(4,128)(2,1)}), bf16[64,3,256]{2,1,0:T(4,128)(2,1)S(1)}, u32[]{:S(2)}, u32[]{:S(2)}) async-start(bf16[64,3,256]{2,1,0:T(4,128)(2,1)} %copy.108), calls=%async_computation.7 | async-start | bytes 262144 | tf_op jit(solution)/shard_map/all_to_all | solution.py:121
  890.5 221.6 %all-to-all-start.9 = ((bf16[64,3,256]{2,1,0:T(4,128)(2,1)}), bf16[64,3,256]{2,1,0:T(4,128)(2,1)S(1)}, u32[]{:S(2)}, u32[]{:S(2)}) async-start(bf16[64,3,256]{2,1,0:T(4,128)(2,1)} %copy.114), calls=%async_computation.13 | async-start | bytes 262144 | tf_op jit(solution)/shard_map/all_to_all | solution.py:151
  899.4 220.3 %copy-start.16 = (f32[64]{0:T(128)S(1)}, f32[64]{0:T(128)}, u32[]{:S(2)}) copy-start(f32[64]{0:T(128)} %copy-done.15) | copy-start | bytes 772
  899.4 220.6 %copy-start.14 = (f32[64]{0:T(128)S(1)}, f32[64]{0:T(128)}, u32[]{:S(2)}) copy-start(f32[64]{0:T(128)} %copy-done.13) | copy-start | bytes 772
  899.4 241.2 %copy-start.20 = (f32[64]{0:T(128)S(1)}, f32[64]{0:T(128)}, u32[]{:S(2)}) copy-start(f32[64]{0:T(128)} %copy-done.19) | copy-start | bytes 772
  899.4 241.4 %copy-start.18 = (f32[64]{0:T(128)S(1)}, f32[64]{0:T(128)}, u32[]{:S(2)}) copy-start(f32[64]{0:T(128)} %copy-done.17) | copy-start | bytes 772
  1112.1 22.1 %all-to-all-start.3 = ((bf16[64,3,256]{2,1,0:T(4,128)(2,1)}), bf16[64,3,256]{2,1,0:T(4,128)(2,1)S(1)}, u32[]{:S(2)}, u32[]{:S(2)}) async-start(bf16[64,3,256]{2,1,0:T(4,128)(2,1)} %copy.102), calls=%async_computation.4 | async-start | bytes 262144 | tf_op jit(solution)/shard_map/all_to_all | solution.py:121
  1134.3 20.6 %all-to-all-start.7 = ((bf16[64,3,256]{2,1,0:T(4,128)(2,1)}), bf16[64,3,256]{2,1,0:T(4,128)(2,1)S(1)}, u32[]{:S(2)}, u32[]{:S(2)}) async-start(bf16[64,3,256]{2,1,0:T(4,128)(2,1)} %copy.111), calls=%async_computation.10 | async-start | bytes 262144 | tf_op jit(solution)/shard_map/all_to_all | solution.py:151
  (14 other events, 116.3 us)
Sparse Core Ops, SparseCore 0:
  651.1 126.9 reduce-scatter.6
  782.6 106.2 reduce-scatter.10
  893.4 106.3 reduce-scatter.4
  1004.2 106.1 reduce-scatter.8
where the time goes:
time: 1170 us; the launch traced here: 1160 us
  waiting for transfers between devices  621 us (53%)
  starting transfers between devices  191 us (16%)
  blocking collectives  177 us (15%)
  local copies, waits for them, and re-layouts  78.7 us (7%)
  other arithmetic  59.2 us (5%)
  matrix products  21.6 us (2%)
  between operations  14.9 us (1%)
    reduce_scatter x2, waiting for transfers between devices, per_device(): lax.psum_scatter(partial_in.reshape(experts, capacity, model_width).astyp...  211 us
    reduce_scatter x2, waiting for transfers between devices, per_device(): lax.psum_scatter(partial_out.reshape(experts, capacity, model_width).asty...  130 us
    all_to_all x1, waiting for transfers between devices, relocate_state(): lax.all_to_all(picked, 'expert', split_axis=0, concat_axis=0, tiled=True)  116 us
    all_gather x1, blocking collectives, per_device(): lax.all_gather(tokens, 'dp', axis=2, tiled=True)  108 us
    all_to_all x2, waiting for transfers between devices, per_device(): lax.all_to_all(row_grads.reshape(experts, capacity, send_width), 'expert'...  92.6 us
    all_to_all x2, starting transfers between devices, per_device(): lax.all_to_all(row_grads.reshape(experts, capacity, send_width), 'expert'...  69.5 us
    all_gather x1, blocking collectives, per_device(): lax.all_gather(cotangent, 'dp', axis=2, tiled=True)  69.5 us
    all_to_all x2, starting transfers between devices, per_device(): lax.all_to_all(row_tokens.reshape(experts, capacity, send_width), 'expert...  67.1 us
  transfers between devices with their start and end apart: 14, of which 11 were waited for; matrix products, arithmetic and copies ran while one was open for 9% of the time, Pallas kernels for 0%

commit v1 on v0

v1 whole, which is shorter than its diff:
```python
import functools

import jax
import jax.numpy as jnp
from jax import lax
from jax.experimental import pallas as pl
from jax.experimental.pallas import tpu as pltpu
from jax.sharding import PartitionSpec as P

MESH = pl.DeviceIdType.MESH
CAP = 3
NX = 4
first_first = (((0,), (0,)), ((), ()))
last_last = (((1,), (1,)), ((), ()))


def mm(a, b, dims=(((1,), (0,)), ((), ()))):
    return lax.dot_general(a, b, dims, preferred_element_type=jnp.float32)


def expert_kernel(
    x_ref, wgu_ref, wd_ref, y_ref, dg_ref,
    full, part, came, zout, zin, acc, dacc, hid, gate_s, up_s,
    z_send, z_recv, x_send, x_recv, own_sem, r_send, r_recv, q_send, q_recv,
):
    width = x_ref.shape[2]
    chunks = x_ref.shape[0]
    dp = lax.axis_index("dp")
    x, zh = dp // 2, dp % 2
    other = x * 2 + (1 - zh)
    peers = [((x + k) % NX) * 2 + zh for k in range(1, NX)]

    def cols(index, size):
        return pl.ds(pl.multiple_of(index * size, size), size)

    barrier = pltpu.get_barrier_semaphore()
    for dev in peers + [other]:
        pl.semaphore_signal(barrier, inc=1, device_id={"dp": dev}, device_id_type=MESH)
    pl.semaphore_wait(barrier, NX)

    def remote(src, dst, send, recv, dev):
        return pltpu.make_async_remote_copy(
            src_ref=src, dst_ref=dst, send_sem=send, recv_sem=recv,
            device_id={"dp": dev}, device_id_type=MESH,
        )

    zc, xc, oc = [], [], []
    for c in range(chunks):
        mine = full.at[c, :, cols(dp, width)]
        cp = remote(x_ref.at[c], mine, z_send.at[c], z_recv.at[c], other)
        cp.start()
        zc.append(cp)
        row = []
        for k, dev in enumerate(peers):
            cp = remote(x_ref.at[c], mine, x_send.at[c, 0, k], x_recv.at[c, 0, k], dev)
            cp.start()
            row.append(cp)
        xc.append(row)
        cp = pltpu.make_async_copy(x_ref.at[c], mine, own_sem.at[c])
        cp.start()
        oc.append(cp)
    for c in range(chunks):
        zc[c].wait_recv()
        theirs = full.at[c, :, cols(other, width)]
        for k, dev in enumerate(peers):
            cp = remote(theirs, theirs, x_send.at[c, 1, k], x_recv.at[c, 1, k], dev)
            cp.start()
            xc[c].append(cp)

    rc, qc = [None] * chunks, [None] * chunks

    def arrive(c):
        oc[c].wait()
        for cp in xc[c]:
            cp.wait_recv()

    def scatter(c):
        rc[c] = []
        for k in range(1, NX):
            to = (x + k) % NX
            cp = remote(
                part.at[c, :, cols(to, 2 * width)], came.at[c, k - 1],
                r_send.at[c, k - 1], r_recv.at[c, k - 1], peers[k - 1],
            )
            cp.start()
            rc[c].append(cp)

    def reduce_x(c):
        for cp in rc[c]:
            cp.wait_recv()
        for half in range(2):
            here = part[c, :, cols(x * 2 + half, width)].astype(jnp.float32)
            for k in range(NX - 1):
                here = here + came[c, k, :, half * width:(half + 1) * width].astype(jnp.float32)
            acc[c, half] = here
        zout[c] = acc[c, 1 - zh].astype(jnp.bfloat16)
        qc[c] = remote(zout.at[c], zin.at[c], q_send.at[c], q_recv.at[c], other)
        qc[c].start()

    def forward(m):
        c = 2 * m
        arrive(c)
        both = mm(full[c], wgu_ref[...])
        hidden_part = both.shape[1] // 2
        gate, up = both[:, :hidden_part], both[:, hidden_part:]
        gate_s[m] = gate
        up_s[m] = up
        hid[m] = (gate * (1.0 / (1.0 + jnp.exp(-gate))) * up).astype(jnp.bfloat16)
        part[c] = mm(hid[m], wd_ref[...]).astype(jnp.bfloat16)
        scatter(c)

    def backward(m):
        c = 2 * m + 1
        arrive(c)
        gate, up = gate_s[m], up_s[m]
        sig = 1.0 / (1.0 + jnp.exp(-gate))
        hidden_grad = mm(full[c], wd_ref[...], last_last)
        gate_grad = hidden_grad * up * sig * (1.0 + gate * (1.0 - sig))
        up_grad = hidden_grad * gate * sig
        both_grad = jnp.concatenate([gate_grad, up_grad], axis=1).astype(jnp.bfloat16)
        part[c] = mm(both_grad, wgu_ref[...], last_last).astype(jnp.bfloat16)
        scatter(c)
        dgrad = mm(hid[m], full[c], first_first)
        if m == 0:
            dacc[...] = dgrad
        else:
            dg_ref[...] = (dacc[...] + dgrad).astype(jnp.bfloat16)

    forward(0)
    backward(0)
    reduce_x(0)
    forward(1)
    reduce_x(1)
    backward(1)
    reduce_x(2)
    reduce_x(3)
    for c in range(chunks):
        qc[c].wait_recv()
        y_ref[c] = (acc[c, zh] + zin[c].astype(jnp.float32)).astype(jnp.bfloat16)
    for c in range(chunks):
        zc[c].wait_send()
        qc[c].wait_send()
        for cp in xc[c] + rc[c]:
            cp.wait_send()


def expert_call(x, wgu, wd):
    chunks, rows, width = x.shape
    model, hidden2 = wgu.shape
    hidden = hidden2 // 2
    bf, f32 = jnp.bfloat16, jnp.float32
    dma = pltpu.SemaphoreType.DMA
    flops = 2 * rows * model * hidden * 2 * 7
    vmem = pl.BlockSpec(memory_space=pltpu.VMEM)
    return pl.pallas_call(
        expert_kernel,
        out_shape=(
            jax.ShapeDtypeStruct((chunks, rows, width), bf),
            jax.ShapeDtypeStruct((hidden, model), bf),
        ),
        in_specs=[vmem] * 3,
        out_specs=(vmem, vmem),
        scratch_shapes=[
            pltpu.VMEM((chunks, rows, model), bf),
            pltpu.VMEM((chunks, rows, model), bf),
            pltpu.VMEM((chunks, NX - 1, rows, 2 * width), bf),
            pltpu.VMEM((chunks, rows, width), bf),
            pltpu.VMEM((chunks, rows, width), bf),
            pltpu.VMEM((chunks, 2, rows, width), f32),
            pltpu.VMEM((hidden, model), f32),
            pltpu.VMEM((2, rows, hidden), bf),
            pltpu.VMEM((2, rows, hidden), f32),
            pltpu.VMEM((2, rows, hidden), f32),
            dma((chunks,)), dma((chunks,)),
            dma((chunks, 2, NX - 1)), dma((chunks, 2, NX - 1)),
            dma((chunks,)),
            dma((chunks, NX - 1)), dma((chunks, NX - 1)),
            dma((chunks,)), dma((chunks,)),
        ],
        compiler_params=pltpu.CompilerParams(
            collective_id=0, has_side_effects=True, vmem_limit_bytes=40 << 20
        ),
        cost_estimate=pl.CostEstimate(flops=flops, bytes_accessed=200 << 20, transcendentals=0),
        name="expert",
    )(x, wgu, wd)


def swap_over(value):
    return lax.all_to_all(value, "expert", split_axis=0, concat_axis=0, tiled=True)


def relocate(flat, source):
    return swap_over(jnp.take(swap_over(flat), source, axis=0))


def per_device(
    tokens, cotangent, routes, gates, source, w_gate_up, w_down, moment_first, moment_second
):
    experts = lax.axis_size("expert")
    micro, count, width = tokens.shape
    model = w_gate_up.shape[1]
    hidden = w_gate_up.shape[3]
    top = routes.shape[2]
    slots = experts * CAP
    bf, f32 = jnp.bfloat16, jnp.float32

    chosen = routes.reshape(micro, count * top)
    earlier = jnp.tri(count * top, k=-1, dtype=bool)
    position = jnp.sum(
        ((chosen[:, :, None] == chosen[:, None, :]) & earlier).astype(jnp.int32), axis=2
    )
    slot_of = (chosen * CAP + position).reshape(micro, count, top)
    slot_ids = jnp.arange(slots, dtype=jnp.int32)
    match = slot_of[..., None] == slot_ids
    picks = match.astype(bf)
    plain = jnp.any(match, axis=2).astype(bf)
    slot_gate = jnp.sum(jnp.where(match, gates[..., None], 0.0), axis=(1, 2))

    rows = []
    for m in range(micro):
        rows.append(mm(plain[m], tokens[m], first_first).astype(bf))
        rows.append((mm(plain[m], cotangent[m], first_first) * slot_gate[m][:, None]).astype(bf))
    send = jnp.stack([r.reshape(experts, CAP, width) for r in rows], axis=1)
    arrived = swap_over(send)
    x = jnp.transpose(arrived, (1, 0, 2, 3)).reshape(2 * micro, slots, width)

    wgu = w_gate_up.reshape(model, 2 * hidden)
    wd = w_down.reshape(hidden, model)
    y, dg = expert_call(x, wgu, wd)

    back = jnp.transpose(y.reshape(2 * micro, experts, CAP, width), (1, 0, 2, 3))
    ret = jnp.transpose(swap_over(back), (1, 0, 2, 3)).reshape(2 * micro, slots, width)
    layer_out, token_grad = [], []
    for m in range(micro):
        out = jnp.zeros((count, width), f32)
        grad = jnp.zeros((count, width), f32)
        for k in range(top):
            out = out + gates[m][:, k:k + 1] * mm(picks[m, :, k], ret[2 * m])
            grad = grad + mm(picks[m, :, k], ret[2 * m + 1])
        layer_out.append(out.astype(bf))
        token_grad.append(grad.astype(bf))

    shares = (experts, hidden // experts, model)
    moments = jnp.concatenate([moment_first.reshape(shares), moment_second.reshape(shares)], axis=1)
    moments = relocate(moments, source)
    down_grad = relocate(dg.reshape(shares), source).reshape(hidden, model).astype(f32)
    half = hidden // experts
    first = 0.9 * moments[:, :half].reshape(hidden, model).astype(f32) + 0.1 * down_grad
    second = (
        0.999 * moments[:, half:].reshape(hidden, model).astype(f32)
        + 0.001 * down_grad * down_grad
    )
    update = first / (jnp.sqrt(second) + 1e-08)
    shape = moment_first.shape
    return (
        jnp.stack(layer_out),
        jnp.stack(token_grad),
        update.astype(bf).reshape(shape),
        first.astype(bf).reshape(shape),
        second.astype(bf).reshape(shape),
    )


def solution(mesh):
    placed = (
        P(None, "expert", "dp"),
        P(None, "expert", "dp"),
        P(None, "expert", None),
        P(None, "expert", None),
        P(),
        P("expert", None, None, "dp"),
        P("expert", "dp", None),
        P("expert", "dp", None),
        P("expert", "dp", None),
    )
    return jax.shard_map(
        per_device,
        mesh=mesh,
        in_specs=placed,
        out_specs=(
            P(None, "expert", "dp"),
            P(None, "expert", "dp"),
            P("expert", "dp", None),
            P("expert", "dp", None),
            P("expert", "dp", None),
        ),
        check_vma=False,
    )
```

time: 1170 us -> 385 us (0.33)
  waiting for transfers between devices: 621 us -> 195 us
  blocking collectives: 177 us -> 0 us
  starting transfers between devices: 191 us -> 57.4 us
  Pallas kernels: 0 us -> 97.9 us
  local copies, waits for them, and re-layouts: 78.7 us -> 15.6 us
  other arithmetic: 59.2 us -> 12.8 us
  matrix products: 21.6 us -> 4.37 us
  between operations: 14.9 us -> 1.02 us
    reduce_scatter x4 -> x0, waiting for transfers between devices: 341 us -> none  [the longest x2 211 us: per_device(): lax.psum_scatter(partial_in.reshape(experts, capacity, model_width).astyp...]
    all_gather x2 -> x0, blocking collectives: 177 us -> none  [the longest x1 108 us: per_device(): lax.all_gather(tokens, 'dp', axis=2, tiled=True)]
    all_to_all x10 -> x6, starting transfers between devices: 191 us -> 57.4 us  [swap_over(): lax.all_to_all(value, 'expert', split_axis=0, concat_axis=0, tiled=True)]
    pallas_call x0 -> x1, Pallas kernels: none -> 97.9 us  [expert_call(): pl.pallas_call(expert_kernel, out_shape=(jax.ShapeDtypeStruct((chunks, ro...]
    all_to_all x10 -> x6, waiting for transfers between devices: 280 us -> 195 us  [swap_over(): lax.all_to_all(value, 'expert', split_axis=0, concat_axis=0, tiled=True)]
    all_to_all x2 -> x0, other arithmetic: 31.6 us -> none  [the longest x1 16.1 us: relocate_state(): lax.all_to_all(flattened, 'expert', split_axis=0, concat_axis=0, tiled=True)]
    unnamed x56 -> x20, local copies, waits for them, and re-layouts: 32.2 us -> 0.96 us
    dot_general x22 -> x12, matrix products: 21.6 us -> 4.37 us  [mm(): return lax.dot_general(a, b, dims, preferred_element_type=jnp.float32)]
  transfers between devices with their start and end apart: 14 -> 6, of which waited for: 11 -> 6; matrix products, arithmetic and copies ran while one was open for 9% -> 4% of each run, Pallas kernels for 0% -> 0%
where the time goes in v1:
time: 385 us; the launch traced here: 384 us
  waiting for transfers between devices  195 us (51%)
  Pallas kernels  97.9 us (25%)
  starting transfers between devices  57.4 us (15%)
  local copies, waits for them, and re-layouts  15.6 us (4%)
  other arithmetic  12.8 us (3%)
  matrix products  4.37 us (1%)
    all_to_all x6, waiting for transfers between devices, swap_over(): lax.all_to_all(value, 'expert', split_axis=0, concat_axis=0, tiled=True)  195 us
    pallas_call x1, Pallas kernels, expert_call(): pl.pallas_call(expert_kernel, out_shape=(jax.ShapeDtypeStruct((chunks, ro...  97.9 us
    all_to_all x6, starting transfers between devices, swap_over(): lax.all_to_all(value, 'expert', split_axis=0, concat_axis=0, tiled=True)  57.4 us
  transfers between devices with their start and end apart: 6, of which 6 were waited for; matrix products, arithmetic and copies ran while one was open for 4% of the time, Pallas kernels for 0%

profile of v1, /device:TPU:1, one launch (start us, length us, event | category | flops | bytes accessed | tf_op | source)
XLA Modules:
  0.0 383.8 jit_solution(7778016264774654370)
XLA Ops:
  7.7 1.3 copy.39
  9.0 17.2 %all-to-all-start = ((bf16[64,4,3,256]{3,1,2,0:T(4,128)(2,1)}), bf16[64,4,3,256]{3,1,2,0:T(4,128)(2,1)S(1)}, u32[]{:S(2)}, u32[]{:S(2)}) async-start(bf16[64,4,3,256]{3,1,2,0:T(4,128)(2,1)} %copy.39), calls=%async_computation | async-start | bytes 786432 | tf_op jit(solution)/shard_map/all_to_all | solution.py:189
  26.4 24.3 %all-to-all-done = bf16[64,4,3,256]{3,1,2,0:T(4,128)(2,1)S(1)} async-done(((bf16[64,4,3,256]{3,1,2,0:T(4,128)(2,1)}), bf16[64,4,3,256]{3,1,2,0:T(4,128)(2,1)S(1)}, u32[]{:S(2)}, u32[]{:S(2)}) %all-to-all-start) | async-done | bytes 393248 | tf_op jit(solution)/shard_map/all_to_all | solution.py:189
  50.7 97.9 %expert.1 = (bf16[4,192,256]{2,1,0:T(8,128)(2,1)S(1)}, bf16[128,2048]{1,0:T(8,128)(2,1)S(1)}) custom-call(bf16[4,192,256]{2,1,0:T(8,128)(2,1)S(1)} %copy.40.x_ref, bf16[2048,256]{1,0:T(8,128)(2,1)S(1)} %bitcast.79, bf16[128,2048]{1,0:T(8,128)(2,1)S(1)} %bitcast.80), custom_call_target="tpu_custom_call" | custom-call | flops 1409286144 | bytes 209715200 | tf_op jit(solution)/shard_map/expert/pallas_call | solution.py:155
  149.6 9.9 %all-to-all-start.1 = ((bf16[64,4,3,256]{3,1,2,0:T(4,128)(2,1)}), bf16[64,4,3,256]{3,1,2,0:T(4,128)(2,1)S(1)}, u32[]{:S(2)}, u32[]{:S(2)}) async-start(bf16[64,4,3,256]{3,1,2,0:T(4,128)(2,1)} %bitcast.15), calls=%async_computation.1 | async-start | bytes 786432 | tf_op jit(solution)/shard_map/all_to_all | solution.py:189
  160.7 23.3 %all-to-all-done.1 = bf16[64,4,3,256]{3,1,2,0:T(4,128)(2,1)S(1)} async-done(((bf16[64,4,3,256]{3,1,2,0:T(4,128)(2,1)}), bf16[64,4,3,256]{3,1,2,0:T(4,128)(2,1)S(1)}, u32[]{:S(2)}, u32[]{:S(2)}) %all-to-all-start.1) | async-done | bytes 393248 | tf_op jit(solution)/shard_map/all_to_all | solution.py:189
  184.0 7.2 %all-to-all-start.4 = ((bf16[64,2,2048]{2,1,0:T(2,128)(2,1)}), bf16[64,2,2048]{2,1,0:T(2,128)(2,1)S(1)}, u32[]{:S(2)}, u32[]{:S(2)}) async-start(bf16[64,2,2048]{2,1,0:T(2,128)(2,1)} %reshape.175), calls=%async_computation.4 | async-start | bytes 1048576 | tf_op jit(solution)/shard_map/all_to_all | solution.py:189
  191.9 2.1 pad_maximum_fusion
  194.0 26.8 %all-to-all-done.4 = bf16[64,2,2048]{2,1,0:T(2,128)(2,1)S(1)} async-done(((bf16[64,2,2048]{2,1,0:T(2,128)(2,1)}), bf16[64,2,2048]{2,1,0:T(2,128)(2,1)S(1)}, u32[]{:S(2)}, u32[]{:S(2)}) %all-to-all-start.4) | async-done | bytes 524320 | tf_op jit(solution)/shard_map/all_to_all | solution.py:189
  220.8 7.5 %all-to-all-start.2 = ((bf16[64,4,2048]{2,1,0:T(4,128)(2,1)}), bf16[64,4,2048]{2,1,0:T(4,128)(2,1)S(1)}, u32[]{:S(2)}, u32[]{:S(2)}) async-start(bf16[64,4,2048]{2,1,0:T(4,128)(2,1)} %pad_maximum_fusion), calls=%async_computation.2 | async-start | bytes 2097152 | tf_op jit(solution)/shard_map/all_to_all | solution.py:189
  228.3 1.6 gather_fusion.1
  229.9 1.4 broadcast_select_fusion.1
  231.3 48.3 %all-to-all-done.2 = bf16[64,4,2048]{2,1,0:T(4,128)(2,1)S(1)} async-done(((bf16[64,4,2048]{2,1,0:T(4,128)(2,1)}), bf16[64,4,2048]{2,1,0:T(4,128)(2,1)S(1)}, u32[]{:S(2)}, u32[]{:S(2)}) %all-to-all-start.2) | async-done | bytes 1048608 | tf_op jit(solution)/shard_map/all_to_all | solution.py:189
  279.6 8.1 %all-to-all-start.5 = ((bf16[64,2,2048]{2,1,0:T(2,128)(2,1)}), bf16[64,2,2048]{2,1,0:T(2,128)(2,1)S(1)}, u32[]{:S(2)}, u32[]{:S(2)}) async-start(bf16[64,2,2048]{2,1,0:T(2,128)(2,1)} %broadcast_select_fusion.1), calls=%async_computation.5 | async-start | bytes 1048576 | tf_op jit(solution)/shard_map/all_to_all | solution.py:189
  287.7 1.4 gather_fusion
  289.2 1.6 broadcast_select_fusion
  290.8 26.6 %all-to-all-done.5 = bf16[64,2,2048]{2,1,0:T(2,128)(2,1)S(1)} async-done(((bf16[64,2,2048]{2,1,0:T(2,128)(2,1)}), bf16[64,2,2048]{2,1,0:T(2,128)(2,1)S(1)}, u32[]{:S(2)}, u32[]{:S(2)}) %all-to-all-start.5) | async-done | bytes 524320 | tf_op jit(solution)/shard_map/all_to_all | solution.py:189
  317.4 7.5 %all-to-all-start.3 = ((bf16[64,4,2048]{2,1,0:T(4,128)(2,1)}), bf16[64,4,2048]{2,1,0:T(4,128)(2,1)S(1)}, u32[]{:S(2)}, u32[]{:S(2)}) async-start(bf16[64,4,2048]{2,1,0:T(4,128)(2,1)} %broadcast_select_fusion), calls=%async_computation.3 | async-start | bytes 2097152 | tf_op jit(solution)/shard_map/all_to_all | solution.py:189
  324.9 1.9 slice_reduce_fusion.1
  330.7 45.4 %all-to-all-done.3 = bf16[64,4,2048]{2,1,0:T(4,128)(2,1)S(1)} async-done(((bf16[64,4,2048]{2,1,0:T(4,128)(2,1)}), bf16[64,4,2048]{2,1,0:T(4,128)(2,1)S(1)}, u32[]{:S(2)}, u32[]{:S(2)}) %all-to-all-start.3) | async-done | bytes 1048608 | tf_op jit(solution)/shard_map/all_to_all | solution.py:189
  376.1 1.2 convert_multiply_fusion
  377.4 1.7 mul.183
  379.1 1.7 mul.178
  380.8 2.9 fusion.14
  (64 shorter events, 14.0 us)
Async XLA Ops:
  0.6 6.2 %copy-start.7 = (bf16[2,64,256]{2,1,0:T(8,128)(2,1)S(1)}, bf16[2,64,256]{2,1,0:T(8,128)(2,1)}, u32[]{:S(2)}) copy-start(bf16[2,64,256]{2,1,0:T(8,128)(2,1)} %param.10) | copy-start | bytes 196612
  7.7 18.5 %copy-start.3 = (bf16[1,2048,2,128]{3,2,1,0:T(2,128)(2,1)S(1)}, bf16[1,2048,2,128]{3,2,1,0:T(2,128)(2,1)}, u32[]{:S(2)}) copy-start(bf16[1,2048,2,128]{3,2,1,0:T(2,128)(2,1)} %param.14) | copy-start | bytes 3145732
  9.0 41.7 %all-to-all-start = ((bf16[64,4,3,256]{3,1,2,0:T(4,128)(2,1)}), bf16[64,4,3,256]{3,1,2,0:T(4,128)(2,1)S(1)}, u32[]{:S(2)}, u32[]{:S(2)}) async-start(bf16[64,4,3,256]{3,1,2,0:T(4,128)(2,1)} %copy.39), calls=%async_computation | async-start | bytes 786432 | tf_op jit(solution)/shard_map/all_to_all | solution.py:189
  26.2 24.5 %copy-start = (bf16[1,128,2048]{2,1,0:T(8,128)(2,1)S(1)}, bf16[1,128,2048]{2,1,0:T(8,128)(2,1)}, u32[]{:S(2)}) copy-start(bf16[1,128,2048]{2,1,0:T(8,128)(2,1)} %param.15) | copy-start | bytes 1572868
  149.6 34.4 %all-to-all-start.1 = ((bf16[64,4,3,256]{3,1,2,0:T(4,128)(2,1)}), bf16[64,4,3,256]{3,1,2,0:T(4,128)(2,1)S(1)}, u32[]{:S(2)}, u32[]{:S(2)}) async-start(bf16[64,4,3,256]{3,1,2,0:T(4,128)(2,1)} %bitcast.15), calls=%async_computation.1 | async-start | bytes 786432 | tf_op jit(solution)/shard_map/all_to_all | solution.py:189
  159.6 31.6 %copy-start.4 = (bf16[1,128,2048]{2,1,0:T(8,128)(2,1)S(1)}, bf16[1,128,2048]{2,1,0:T(8,128)(2,1)}, u32[]{:S(2)}) copy-start(bf16[1,128,2048]{2,1,0:T(8,128)(2,1)} %param.16) | copy-start | bytes 1572868
  160.7 30.8 %copy-start.5 = (bf16[1,128,2048]{2,1,0:T(8,128)(2,1)S(1)}, bf16[1,128,2048]{2,1,0:T(8,128)(2,1)}, u32[]{:S(2)}) copy-start(bf16[1,128,2048]{2,1,0:T(8,128)(2,1)} %param.17) | copy-start | bytes 1572868
  184.0 36.8 %all-to-all-start.4 = ((bf16[64,2,2048]{2,1,0:T(2,128)(2,1)}), bf16[64,2,2048]{2,1,0:T(2,128)(2,1)S(1)}, u32[]{:S(2)}, u32[]{:S(2)}) async-start(bf16[64,2,2048]{2,1,0:T(2,128)(2,1)} %reshape.175), calls=%async_computation.4 | async-start | bytes 1048576 | tf_op jit(solution)/shard_map/all_to_all | solution.py:189
  194.0 34.3 %copy-start.8 = (s32[64]{0:T(128)S(1)}, s32[64]{0:T(128)}, u32[]{:S(2)}) copy-start(s32[64]{0:T(128)} %param.13) | copy-start | bytes 772
  220.8 58.8 %all-to-all-start.2 = ((bf16[64,4,2048]{2,1,0:T(4,128)(2,1)}), bf16[64,4,2048]{2,1,0:T(4,128)(2,1)S(1)}, u32[]{:S(2)}, u32[]{:S(2)}) async-start(bf16[64,4,2048]{2,1,0:T(4,128)(2,1)} %pad_maximum_fusion), calls=%async_computation.2 | async-start | bytes 2097152 | tf_op jit(solution)/shard_map/all_to_all | solution.py:189
  279.6 37.7 %all-to-all-start.5 = ((bf16[64,2,2048]{2,1,0:T(2,128)(2,1)}), bf16[64,2,2048]{2,1,0:T(2,128)(2,1)S(1)}, u32[]{:S(2)}, u32[]{:S(2)}) async-start(bf16[64,2,2048]{2,1,0:T(2,128)(2,1)} %broadcast_select_fusion.1), calls=%async_computation.5 | async-start | bytes 1048576 | tf_op jit(solution)/shard_map/all_to_all | solution.py:189
  290.8 34.1 %copy-start.6 = (f32[2,64,2]{1,2,0:T(2,128)S(1)}, f32[2,64,2]{1,2,0:T(2,128)}, u32[]{:S(2)}) copy-start(f32[2,64,2]{1,2,0:T(2,128)} %param.12) | copy-start | bytes 3076
  317.4 58.8 %all-to-all-start.3 = ((bf16[64,4,2048]{2,1,0:T(4,128)(2,1)}), bf16[64,4,2048]{2,1,0:T(4,128)(2,1)S(1)}, u32[]{:S(2)}, u32[]{:S(2)}) async-start(bf16[64,4,2048]{2,1,0:T(4,128)(2,1)} %broadcast_select_fusion), calls=%async_computation.3 | async-start | bytes 2097152 | tf_op jit(solution)/shard_map/all_to_all | solution.py:189
  379.1 1.7 copy-start.1
  379.1 1.7 copy-start.2
